TPU v7x, 32 devices: a whole 2x2x4 slice. The times are simulated.
32 devices in a mesh: parts: 1, grid: 32 (over z, y, x, core).
Axes of the slice: x: 2, y: 2, z: 4, core: 2. Of those that a mesh axis runs over, the one named last changes fastest.
Arguments:
- tokens: bfloat16 [128, 32, 1024], P(('parts', 'grid')), may hold values from -6 to 6
- cotangent: bfloat16 [128, 32, 1024], P(('parts', 'grid')), may hold values from -6 to 6
- w_sqkv: bfloat16 [1024, 3072], P('grid'), may hold values from -0.1875 to 0.1875
- w_so: bfloat16 [1024, 1024], P('grid'), may hold values from -0.1875 to 0.1875
- w_gqkv: bfloat16 [1024, 3072], P('grid'), may hold values from -0.1875 to 0.1875
- w_go: bfloat16 [1024, 1024], P('grid'), may hold values from -0.1875 to 0.1875
- keep: int32 [32, 128], P(None, 'parts'), may hold values from 0 to 1, as said below
Outputs:
- mixed: bfloat16 [128, 32, 1024], P(('parts', 'grid'))
- token_grad: bfloat16 [128, 32, 1024], P(('parts', 'grid'))
Inputs may be any that keep to these rules, and one draw needn't show every extreme that they name: `keep`: every band group keeps at least one patch; the kept share differs from group to group.
All inputs are finite; a program needn't handle non-finite values.
Results may differ from a plain program's by a relative error of at most 0.017.
Values may be sent and summed in bfloat16 or wider, within the bound.
A program may use at most 192 MiB of HBM per device.

v0:
```python
from functools import partial

import jax
import jax.numpy as jnp
from jax import lax
from jax.sharding import PartitionSpec as P

H = 16
G = 32


def rms_normalize(values):
    wide = values.astype(jnp.float32)
    meansq = jnp.mean(wide * wide, axis=-1, keepdims=True)
    return (wide * lax.rsqrt(meansq + 1e-06)).astype(jnp.bfloat16)


def project_spatial(tokens, weight):
    patches, groups, width = tokens.shape
    normed = rms_normalize(tokens).reshape(patches * groups, width)
    stacked = jnp.dot(normed, weight, preferred_element_type=jnp.float32).astype(jnp.bfloat16)
    stacked = stacked.reshape(patches, groups, 3, width).transpose(2, 0, 1, 3)
    return stacked.reshape(3, patches, groups * width)


def pair_attention(operands):
    stacked, keep_row = operands
    query, keyed, valued = (stacked[0], stacked[1], stacked[2])
    scale = query.shape[-1] ** (-0.5)
    scores = jnp.dot(query, keyed.T, preferred_element_type=jnp.float32) * scale
    weights = jnp.exp(scores) * keep_row[None, :]
    probs = (weights / jnp.sum(weights, axis=-1, keepdims=True)).astype(jnp.bfloat16)
    return jnp.dot(probs, valued, preferred_element_type=jnp.float32).astype(jnp.bfloat16)


def spatial_attention(stacked, keep_rows, attend):
    three, patches, columns = stacked.shape
    pairs = keep_rows.shape[0]
    split = stacked.reshape(3, patches, pairs, columns // pairs).transpose(2, 0, 1, 3)
    result = lax.map(attend, (split, keep_rows))
    return result.transpose(1, 0, 2).reshape(patches, columns)


def block_group(tokens, attended, w_so, w_gqkv, w_go):
    patches, groups, width = tokens.shape
    rows = patches * groups
    heads = H
    y_first = (
        tokens.reshape(rows, width).astype(jnp.float32)
        + jnp.dot(attended.reshape(rows, width), w_so, preferred_element_type=jnp.float32)
    ).astype(jnp.bfloat16)
    normed = rms_normalize(y_first)
    stacked = jnp.dot(normed, w_gqkv, preferred_element_type=jnp.float32).astype(jnp.bfloat16)
    stacked = stacked.reshape(patches, groups, 3, heads, width // heads)
    query = stacked[:, :, 0].astype(jnp.float32)
    keyed = stacked[:, :, 1].astype(jnp.float32)
    valued = stacked[:, :, 2].astype(jnp.float32)
    scale = (width // heads) ** (-0.5)
    scores = jnp.einsum("pgne,pkne->pngk", query, keyed) * scale
    weights = jnp.exp(scores)
    probs = (weights / jnp.sum(weights, axis=-1, keepdims=True)).astype(jnp.bfloat16)
    result = jnp.einsum("pngk,pkne->pgne", probs.astype(jnp.float32), valued).astype(jnp.bfloat16)
    result = result.reshape(rows, width)
    mixed = (
        y_first.astype(jnp.float32) + jnp.dot(result, w_go, preferred_element_type=jnp.float32)
    ).astype(jnp.bfloat16)
    return mixed.reshape(patches, groups, width)


def local(tokens, cotangent, w_sqkv, w_so, w_gqkv, w_go, keep):
    grid_size = lax.axis_size("grid")
    position = lax.axis_index("grid")
    full_sqkv, full_so, full_gqkv, full_go = (
        lax.all_gather(w_sqkv, "grid", axis=0, tiled=True),
        lax.all_gather(w_so, "grid", axis=0, tiled=True),
        lax.all_gather(w_gqkv, "grid", axis=0, tiled=True),
        lax.all_gather(w_go, "grid", axis=0, tiled=True),
    )
    stacked, pull_first = jax.vjp(partial(project_spatial, weight=full_sqkv), tokens)
    banded = lax.all_to_all(stacked, "grid", split_axis=2, concat_axis=1, tiled=True)
    pairs = G * H // grid_size
    pair_ids = position * pairs + jnp.arange(pairs, dtype=jnp.int32)
    select = (pair_ids[:, None] // H == jnp.arange(G, dtype=jnp.int32)[None, :]).astype(jnp.float32)
    keep_rows = jnp.dot(select, keep.astype(jnp.float32), precision=lax.Precision.HIGHEST)
    attend = jax.checkpoint(pair_attention)
    attended_bands, pull_spatial = jax.vjp(
        partial(spatial_attention, keep_rows=keep_rows, attend=attend), banded
    )
    attended = lax.all_to_all(attended_bands, "grid", split_axis=0, concat_axis=1, tiled=True)
    mixed, pull_group = jax.vjp(
        partial(block_group, w_so=full_so, w_gqkv=full_gqkv, w_go=full_go), tokens, attended
    )
    grad_direct, grad_attended = pull_group(cotangent)
    grad_bands = lax.all_to_all(grad_attended, "grid", split_axis=1, concat_axis=0, tiled=True)
    (grad_banded,) = pull_spatial(grad_bands)
    grad_stacked = lax.all_to_all(grad_banded, "grid", split_axis=1, concat_axis=2, tiled=True)
    (grad_first,) = pull_first(grad_stacked)
    return (mixed, grad_direct + grad_first)


def solution(mesh):
    placed = (
        P(("parts", "grid"), None, None),
        P(("parts", "grid"), None, None),
        P("grid", None),
        P("grid", None),
        P("grid", None),
        P("grid", None),
        P(None, "parts"),
    )
    return jax.shard_map(
        local,
        mesh=mesh,
        in_specs=placed,
        out_specs=(P(("parts", "grid"), None, None), P(("parts", "grid"), None, None)),
        check_vma=False,
    )
```

profile of v0, /device:TPU:0, one launch (start us, length us, event | category | flops | bytes accessed | tf_op | source)
XLA Modules:
  0.0 407.9 jit_solution(649732156367251045)
XLA Ops:
  10.0 1.1 fusion.43
  11.1 1.1 fusion.44
  12.1 70.6 %all-gather.5.cloned.1.call-done = bf16[1024,3072]{1,0:T(8,128)(2,1)} async-done(((bf16[32,3072]{1,0:T(8,128)(2,1)}), bf16[1024,3072]{1,0:T(8,128)(2,1)}) %all-gather.5.cloned.1.call-update) | async-done | bytes 6291472 | tf_op jit(solution)/shard_map/all_gather | solution.py:74
  82.7 3.8 convolution_convert_fusion.6
  86.5 1.2 reshape.171
  87.7 33.8 %copy.75 = bf16[3,4,32,1024]{1,0,3,2:T(4,128)(2,1)} copy(bf16[3,4,32,1024]{3,0,2,1:T(4,128)(2,1)S(1)} %bitcast.189) | data formatting | bytes 1572864 | tf_op jit(solution)/shard_map/jvp()/reshape | solution.py:23
  121.5 36.9 %reshape.187 = bf16[32,2,6144]{2,1,0:T(2,128)(2,1)} reshape(bf16[32768,3,4]{2,1,0:T(4,128)(2,1)} %bitcast.185) | data formatting | bytes 1572864
  158.4 3.0 all-to-all-start
  161.6 23.1 %all-to-all-done = bf16[32,2,6144]{2,1,0:T(2,128)(2,1)S(1)} async-done(((bf16[32,2,6144]{2,1,0:T(2,128)(2,1)}), bf16[32,2,6144]{2,1,0:T(2,128)(2,1)S(1)}, u32[]{:S(2)}, u32[]{:S(2)}) %all-to-all-start) | async-done | bytes 786464 | tf_op jit(solution)/shard_map/all_to_all | solution.py:80
  184.7 31.4 %reshape.188 = bf16[32768,3,4]{2,1,0:T(4,128)(2,1)} reshape(bf16[32,2,6144]{2,1,0:T(2,128)(2,1)S(1)} %all-to-all-done) | data formatting | bytes 1572864
  216.1 42.5 %copy.54 = bf16[3,4,32,1024]{3,1,2,0:T(4,128)(2,1)S(1)} copy(bf16[3,4,32,1024]{1,0,3,2:T(4,128)(2,1)} %bitcast.186) | data formatting | bytes 1572864 | tf_op jit(solution)/shard_map/all_to_all | solution.py:80
  258.6 1.0 reshape.173
  260.1 16.3 %while.24 = (s32[]{:T(128)}, bf16[16,128,64]{1,2,0:T(8,128)(2,1)}, bf16[16,3,128,64]{3,2,1,0:T(8,128)(2,1)S(1)}, f32[16,128]{1,0:T(8,128)S(1)}, s32[]{:T(128)}, /*index=5*/s32[]{:T(128)}, s32[]{}, s32[]{}) while((s32[]{:T(128)}, bf16[16,128,64]{1,2,0:T(8,128)(2,1)}, bf16[16,3,128,64]{3,2,1,0:T(8,128)(2,1)S(1)}, f32[16,128]{1,0:T(8,128)S(1)}, ...), condition=%wide.region_3.4_spmd, body=%wide.region_1.3_spmd.sunk | while | flops 4284292 | bytes 250489 | solution.py:40
  261.3 0.8 fusion.90
  262.3 0.8 fusion.90
  263.3 0.8 fusion.90
  264.3 0.8 fusion.90
  265.4 0.8 fusion.90
  266.4 0.8 fusion.90
  267.4 0.8 fusion.90
  268.4 0.8 fusion.90
  269.4 0.8 fusion.90
  270.4 0.8 fusion.90
  274.5 0.8 fusion.90
  276.3 1.5 copy.56
  277.9 1.0 all_to_all.47
  278.9 4.1 %all-to-all-start.1 = ((bf16[32,4,1024]{2,1,0:T(4,128)(2,1)}), bf16[32,4,1024]{2,1,0:T(4,128)(2,1)S(1)}, u32[]{:S(2)}, u32[]{:S(2)}) async-start(bf16[32,4,1024]{2,1,0:T(4,128)(2,1)} %all_to_all.47), calls=%async_computation.1 | async-start | bytes 524288 | tf_op jit(solution)/shard_map/all_to_all | solution.py:89
  283.0 2.5 convolution_convert_fusion.15
  285.8 7.5 %all-to-all-done.1 = bf16[32,4,1024]{2,1,0:T(4,128)(2,1)S(1)} async-done(((bf16[32,4,1024]{2,1,0:T(4,128)(2,1)}), bf16[32,4,1024]{2,1,0:T(4,128)(2,1)S(1)}, u32[]{:S(2)}, u32[]{:S(2)}) %all-to-all-start.1) | async-done | bytes 262176 | tf_op jit(solution)/shard_map/all_to_all | solution.py:89
  293.5 2.1 multiply_reduce_fusion.3
  295.6 4.7 %convolution_convert_fusion.5 = bf16[128,3072]{1,0:T(8,128)(2,1)} fusion(bf16[1024,3072]{1,0:T(8,128)(2,1)} %all-gather.9.cloned.1.call-done, f32[128,1024]{1,0:T(8,128)S(1)} %get-tuple-element.187, f32[128]{0:T(128)S(1)} %fusion.54), kind=kOutput, calls=%fused_computation.45 | convolution fusion | flops 805961728 | bytes 7602688 | tf_op jit(solution)/shard_map/jvp()/dot_general | solution.py:53
  300.3 2.1 reshape.175
  305.4 1.8 copy.65
  307.1 2.3 reshape.180
  309.4 5.2 %multiply_reduce_fusion.2 = (f32[128]{0:T(128)S(1)}, f32[128,1024]{1,0:T(8,128)S(1)}) fusion(f32[128,1024]{1,0:T(8,128)S(1)} %get-tuple-element.187, bf16[128,3072]{1,0:T(8,128)(2,1)S(1)} %reshape.180, bf16[1024,3072]{1,0:T(8,128)(2,1)} %all-gather.9.cloned.1.call-done), kind=kOutput, calls=%fused_computation.94 | convolution fusion | flops 805830528 | bytes 8126976 | tf_op jit(solution)/shard_map/transpose(jvp())/dot_general | solution.py:53
  314.8 0.8 convolution_convert_fusion.13
  315.9 12.8 %all_to_all.59 = bf16[4,32,1024]{2,0,1:T(4,128)(2,1)S(1)} all-to-all(bf16[4,32,1024]{2,0,1:T(4,128)(2,1)S(1)} %copy.66), channel_id=1, replica_groups=mesh['parts'=1,'grid'=32] {'grid'}, dimensions={1} | all-to-all | bytes 524288 | tf_op jit(solution)/shard_map/all_to_all | solution.py:94
  329.4 32.7 %while.25 = (s32[]{:T(128)}, bf16[16,3,128,64]{2,3,0,1:T(8,128)(2,1)S(1)}, bf16[16,3,128,64]{3,2,1,0:T(8,128)(2,1)}, f32[16,128]{1,0:T(8,128)S(1)}, bf16[16,128,64]{2,1,0:T(8,128)(2,1)S(1)}, /*index=5*/s32[]{:T(128)}, s32[]{:T(128)}) while((s32[]{:T(128)}, bf16[16,3,128,64]{2,3,0,1:T(8,128)(2,1)S(1)}, bf16[16,3,128,64]{3,2,1,0:T(8,128)(2,1)}, ...), condition=%wide.region_11.12_spmd, body=%wide.region_8.11_spmd.sunk | while | flops 11018371 | bytes 1025641 | solution.py:40
  329.4 0.9 dynamic-slice_bitcast_fusion.12
  331.4 0.9 dynamic-slice_bitcast_fusion.12
  333.5 0.9 dynamic-slice_bitcast_fusion.12
  335.5 0.9 dynamic-slice_bitcast_fusion.12
  337.6 0.9 dynamic-slice_bitcast_fusion.12
  339.6 0.9 dynamic-slice_bitcast_fusion.12
  341.7 0.9 dynamic-slice_bitcast_fusion.12
  343.7 0.9 dynamic-slice_bitcast_fusion.12
  345.7 0.9 dynamic-slice_bitcast_fusion.12
  347.8 0.9 dynamic-slice_bitcast_fusion.12
  349.8 0.9 dynamic-slice_bitcast_fusion.12
  351.9 0.9 dynamic-slice_bitcast_fusion.12
  353.9 0.9 dynamic-slice_bitcast_fusion.12
  356.0 0.9 dynamic-slice_bitcast_fusion.12
  358.0 0.9 dynamic-slice_bitcast_fusion.12
  360.0 0.9 dynamic-slice_bitcast_fusion.12
  362.1 1.7 copy.70
  363.8 3.6 all-to-all-start.3
  367.4 1.9 fusion.27
  369.3 1.0 copy.62
  370.3 1.4 reshape.176
  371.8 1.2 fusion.32
  372.9 20.4 %all-to-all-done.3 = bf16[3,128,1024]{2,0,1:T(4,128)(2,1)} async-done(((bf16[3,128,1024]{2,0,1:T(4,128)(2,1)}), bf16[3,128,1024]{2,0,1:T(4,128)(2,1)}, u32[]{:S(2)}, u32[]{:S(2)}) %all-to-all-start.3) | async-done | bytes 786464 | tf_op jit(solution)/shard_map/all_to_all | solution.py:96
  393.3 1.6 copy.72
  395.3 5.0 %convolution_convert_fusion.12 = bf16[128,1024]{1,0:T(8,128)(2,1)S(1)} fusion(bf16[128,3072]{1,0:T(8,128)(2,1)S(1)} %bitcast.191, bf16[1024,3072]{1,0:T(8,128)(2,1)} %all-gather.5.cloned.1.call-done), kind=kOutput, calls=%fused_computation.63 | convolution fusion | flops 805437440 | bytes 7340032 | tf_op jit(solution)/shard_map/transpose(jvp())/dot_general | solution.py:21
  400.4 0.9 fusion.47
  (250 shorter events, 33.0 us)
Async XLA Ops:
  7.2 75.6 %all-gather.5.cloned.1.call-start = ((), (), s32[]{:S(2)}) async-start(), calls=%async_computation.4 | async-start | bytes 6488064 | tf_op jit(solution)/shard_map/all_gather | solution.py:74
  7.9 275.1 %all-gather.11.cloned.1.call-start = ((), (), s32[]{:S(2)}) async-start(), calls=%async_computation.7 | async-start | bytes 2162688 | tf_op jit(solution)/shard_map/all_gather | solution.py:77
  8.6 284.8 %all-gather.7.cloned.1.call-start = ((), (), s32[]{:S(2)}) async-start(), calls=%async_computation.5 | async-start | bytes 2162688 | tf_op jit(solution)/shard_map/all_gather | solution.py:75
  9.4 286.3 %all-gather.9.cloned.1.call-start = ((), (), s32[]{:S(2)}) async-start(), calls=%async_computation.6 | async-start | bytes 6488064 | tf_op jit(solution)/shard_map/all_gather | solution.py:76
  121.5 39.9 %copy-start.7 = (s32[32,128]{1,0:T(8,128)S(1)}, s32[32,128]{1,0:T(8,128)}, u32[]{:S(2)}) copy-start(s32[32,128]{1,0:T(8,128)} %param.17) | copy-start | bytes 49156
  158.4 26.3 %all-to-all-start = ((bf16[32,2,6144]{2,1,0:T(2,128)(2,1)}), bf16[32,2,6144]{2,1,0:T(2,128)(2,1)S(1)}, u32[]{:S(2)}, u32[]{:S(2)}) async-start(bf16[32,2,6144]{2,1,0:T(2,128)(2,1)} %reshape.187), calls=%async_computation | async-start | bytes 1572864 | tf_op jit(solution)/shard_map/all_to_all | solution.py:80
  260.0 23.0 %copy-start.6 = (bf16[4,32,1024]{2,1,0:T(8,128)(2,1)S(1)}, bf16[4,32,1024]{2,1,0:T(8,128)(2,1)}, u32[]{:S(2)}) copy-start(bf16[4,32,1024]{2,1,0:T(8,128)(2,1)} %param.12) | copy-start | bytes 786436
  276.3 2.5 copy-start.4
  278.9 14.5 %all-to-all-start.1 = ((bf16[32,4,1024]{2,1,0:T(4,128)(2,1)}), bf16[32,4,1024]{2,1,0:T(4,128)(2,1)S(1)}, u32[]{:S(2)}, u32[]{:S(2)}) async-start(bf16[32,4,1024]{2,1,0:T(4,128)(2,1)} %all_to_all.47), calls=%async_computation.1 | async-start | bytes 524288 | tf_op jit(solution)/shard_map/all_to_all | solution.py:89
  283.0 10.5 %copy-start.2 = (bf16[4,32,1024]{2,1,0:T(8,128)(2,1)S(1)}, bf16[4,32,1024]{2,1,0:T(8,128)(2,1)}, u32[]{:S(2)}) copy-start(bf16[4,32,1024]{2,1,0:T(8,128)(2,1)} %param.11) | copy-start | bytes 786436
  302.8 0.8 copy-start.5
  303.3 1.2 copy-start.3
  309.4 5.4 %copy-start.1 = (bf16[1024,1024]{1,0:T(8,128)(2,1)S(1)}, bf16[1024,1024]{1,0:T(8,128)(2,1)}, u32[]{:S(2)}) copy-start(bf16[1024,1024]{1,0:T(8,128)(2,1)} %all-gather.7.cloned.1.call-done) | copy-start | bytes 6291460
  363.8 29.6 %all-to-all-start.3 = ((bf16[3,128,1024]{2,0,1:T(4,128)(2,1)}), bf16[3,128,1024]{2,0,1:T(4,128)(2,1)}, u32[]{:S(2)}, u32[]{:S(2)}) async-start(bf16[3,128,1024]{2,0,1:T(4,128)(2,1)} %copy.70), calls=%async_computation.3 | async-start | bytes 2097152 | tf_op jit(solution)/shard_map/all_to_all | solution.py:96
  367.4 4.4 %copy-start = (bf16[1024,1024]{1,0:T(8,128)(2,1)S(1)}, bf16[1024,1024]{1,0:T(8,128)(2,1)}, u32[]{:S(2)}) copy-start(bf16[1024,1024]{1,0:T(8,128)(2,1)} %all-gather.11.cloned.1.call-done) | copy-start | bytes 6291460
Sparse Core Ops, SparseCore 0:
  10.8 71.8 all-gather.4
  85.6 54.7 all-gather.10
  143.2 56.5 all-gather.6
  202.6 67.9 all-gather.8
where the time goes:
time: 411 us; the launch traced here: 408 us
  local copies, waits for them, and re-layouts  178 us (43%)
  waiting for transfers between devices  124 us (30%)
  matrix products  62.1 us (15%)
  between operations  14.2 us (3%)
  blocking collectives  12.8 us (3%)
  starting transfers between devices  10.8 us (3%)
  other arithmetic  4.5 us (1%)
    all_gather x1, waiting for transfers between devices, local(): lax.all_gather(w_sqkv, 'grid', axis=0, tiled=True)  70.6 us
    unnamed x19, local copies, waits for them, and re-layouts  68.7 us
    all_to_all x1, local copies, waits for them, and re-layouts, local(): lax.all_to_all(stacked, 'grid', split_axis=2, concat_axis=1, tiled=True)  42.5 us
    reshape x1, local copies, waits for them, and re-layouts, project_spatial(): return stacked.reshape(3, patches, groups * width)  33.8 us
    all_to_all x1, waiting for transfers between devices, local(): lax.all_to_all(stacked, 'grid', split_axis=2, concat_axis=1, tiled=True)  23.1 us
    all_to_all x1, waiting for transfers between devices, local(): lax.all_to_all(grad_banded, 'grid', split_axis=1, concat_axis=2, tiled=True)  20.4 us
    dot_general x48, matrix products, pair_attention(): jnp.dot(probs, valued, preferred_element_type=jnp.float32)  19.4 us
    squeeze x48, local copies, waits for them, and re-layouts, spatial_attention(): result = lax.map(attend, (split, keep_rows))  14.7 us
  transfers between devices with their start and end apart: 7, of which 4 were waited for; matrix products, arithmetic and copies ran while one was open for 45% of the time, Pallas kernels for 0%

commit v1 on v0

--- a/solution.py
+++ b/solution.py
@@ -3,6 +3,8 @@
 import jax
 import jax.numpy as jnp
 from jax import lax
+from jax.experimental import pallas as pl
+from jax.experimental.pallas import tpu as pltpu
 from jax.sharding import PartitionSpec as P
 
 H = 16
@@ -67,7 +69,7 @@
     return mixed.reshape(patches, groups, width)
 
 
-def local(tokens, cotangent, w_sqkv, w_so, w_gqkv, w_go, keep):
+def local_any(tokens, cotangent, w_sqkv, w_so, w_gqkv, w_go, keep):
     grid_size = lax.axis_size("grid")
     position = lax.axis_index("grid")
     full_sqkv, full_so, full_gqkv, full_go = (
@@ -98,6 +100,250 @@
     return (mixed, grad_direct + grad_first)
 
 
+F32 = jnp.float32
+BF16 = jnp.bfloat16
+LANES = 128
+EPS = 1e-06
+
+
+def nn(a, b):
+    return lax.dot_general(a, b, (((1,), (0,)), ((), ())), preferred_element_type=F32)
+
+
+def nt(a, b):
+    return lax.dot_general(a, b, (((1,), (1,)), ((), ())), preferred_element_type=F32)
+
+
+def tn(a, b):
+    return lax.dot_general(a, b, (((0,), (0,)), ((), ())), preferred_element_type=F32)
+
+
+def rms_parts(wide):
+    inv = lax.rsqrt(jnp.mean(wide * wide, axis=-1, keepdims=True) + EPS)
+    return inv, (wide * inv).astype(BF16)
+
+
+def rms_pull(wide, inv, grad):
+    inner = jnp.mean(grad * wide, axis=-1, keepdims=True)
+    return grad * inv - wide * (inv * inv * inv * inner)
+
+
+def halves(head):
+    lane = lax.broadcasted_iota(jnp.int32, (1, LANES), 1)
+    parts = []
+    for index in range(LANES // head):
+        parts.append((lane // head == index).astype(F32))
+    return parts
+
+
+def merge(selects, parts):
+    total = parts[0] * selects[0]
+    for select, part in zip(selects[1:], parts[1:]):
+        total = total + part * select
+    return total.astype(BF16)
+
+
+def head_probs(query, keyed, select, mask, scale):
+    scores = nt(query * select.astype(BF16), keyed) * scale
+    weights = jnp.where(mask, jnp.exp(scores), 0.0)
+    return weights * (1.0 / jnp.sum(weights, axis=-1, keepdims=True))
+
+
+def head_pull(probs, query, keyed, valued, grad, select, scale):
+    dprobs = nt(grad * select.astype(BF16), valued).astype(BF16).astype(F32)
+    inner = jnp.sum(dprobs * probs, axis=-1, keepdims=True)
+    dscores = (probs * (dprobs - inner) * scale).astype(BF16)
+    return nn(dscores, keyed), tn(dscores, query), tn(probs.astype(BF16), grad)
+
+
+def columns_of(qkv_ref, width, block):
+    at = block * LANES
+    return tuple(qkv_ref[:, part * width + at : part * width + at + LANES] for part in range(3))
+
+
+def spatial_kernel(head, x_ref, w_ref, w_so_ref, keep_ref, qkv_ref, y_ref, att_ref):
+    width = x_ref.shape[1]
+    _, normed = rms_parts(x_ref[...].astype(F32))
+    tile = 512
+    for at in range(0, 3 * width, tile):
+        qkv_ref[:, at : at + tile] = nn(normed, w_ref[:, at : at + tile]).astype(BF16)
+    rows = x_ref.shape[0]
+    mask = jnp.broadcast_to(keep_ref[...], (rows, rows)) > 0.0
+    selects = halves(head)
+    scale = head ** (-0.5)
+    for block in range(width // LANES):
+        query, keyed, valued = columns_of(qkv_ref, width, block)
+        parts = []
+        for select in selects:
+            probs = head_probs(query, keyed, select, mask, scale)
+            parts.append(nn(probs.astype(BF16), valued))
+        att_ref[:, block * LANES : (block + 1) * LANES] = merge(selects, parts)
+    attended = att_ref[...]
+    for at in range(0, width, tile):
+        y_ref[:, at : at + tile] = (
+            x_ref[:, at : at + tile].astype(F32) + nn(attended, w_so_ref[:, at : at + tile])
+        ).astype(BF16)
+
+
+def spatial_pull_kernel(
+    head, dy_ref, x_ref, qkv_ref, keep_ref, w_so_ref, w_ref, out_ref, datt_ref, dqkv_ref
+):
+    rows, width = x_ref.shape
+    dy = dy_ref[...]
+    tile = 512
+    for at in range(0, width, tile):
+        datt_ref[:, at : at + tile] = nt(dy, w_so_ref[at : at + tile, :]).astype(BF16)
+    mask = jnp.broadcast_to(keep_ref[...], (rows, rows)) > 0.0
+    selects = halves(head)
+    scale = head ** (-0.5)
+    for block in range(width // LANES):
+        query, keyed, valued = columns_of(qkv_ref, width, block)
+        at = block * LANES
+        grad = datt_ref[:, at : at + LANES]
+        pulled = []
+        for select in selects:
+            probs = head_probs(query, keyed, select, mask, scale)
+            pulled.append(head_pull(probs, query, keyed, valued, grad, select, scale))
+        for part in range(3):
+            dqkv_ref[:, part * width + at : part * width + at + LANES] = merge(
+                selects, [pull[part] for pull in pulled]
+            )
+    wide = x_ref[...].astype(F32)
+    inv, _ = rms_parts(wide)
+    dqkv = dqkv_ref[...]
+    for at in range(0, width, tile):
+        datt_ref[:, at : at + tile] = nt(dqkv, w_ref[at : at + tile, :]).astype(BF16)
+    first = rms_pull(wide, inv, datt_ref[...].astype(F32)).astype(BF16)
+    out_ref[...] = dy + first
+
+
+def group_kernel(
+    head, patches, y_ref, c_ref, w_ref, w_go_ref, mixed_ref, dy_ref, qkv_ref, att_ref, datt_ref
+):
+    rows, width = y_ref.shape
+    groups = rows // patches
+    row = lax.broadcasted_iota(jnp.int32, (rows, rows), 0)
+    col = lax.broadcasted_iota(jnp.int32, (rows, rows), 1)
+    turn = (col == (row % groups) * patches + row // groups).astype(F32).astype(BF16)
+    mask = (row // groups) == (col // groups)
+    y_first = nn(turn, y_ref[...])
+    inv, normed = rms_parts(y_first)
+    cot = c_ref[...]
+    tile = 512
+    for at in range(0, 3 * width, tile):
+        qkv_ref[:, at : at + tile] = nn(normed, w_ref[:, at : at + tile]).astype(BF16)
+    for at in range(0, width, tile):
+        datt_ref[:, at : at + tile] = nt(cot, w_go_ref[at : at + tile, :]).astype(BF16)
+    selects = halves(head)
+    scale = head ** (-0.5)
+    for block in range(width // LANES):
+        query, keyed, valued = columns_of(qkv_ref, width, block)
+        at = block * LANES
+        grad = datt_ref[:, at : at + LANES]
+        parts, pulled = [], []
+        for select in selects:
+            probs = head_probs(query, keyed, select, mask, scale)
+            parts.append(nn(probs.astype(BF16), valued))
+            pulled.append(head_pull(probs, query, keyed, valued, grad, select, scale))
+        att_ref[:, at : at + LANES] = merge(selects, parts)
+        for part in range(3):
+            qkv_ref[:, part * width + at : part * width + at + LANES] = merge(
+                selects, [pull[part] for pull in pulled]
+            )
+    attended = att_ref[...]
+    for at in range(0, width, tile):
+        mixed_ref[:, at : at + tile] = (
+            y_first[:, at : at + tile] + nn(attended, w_go_ref[:, at : at + tile])
+        ).astype(BF16)
+    dqkv = qkv_ref[...]
+    for at in range(0, width, tile):
+        datt_ref[:, at : at + tile] = nt(dqkv, w_ref[at : at + tile, :]).astype(BF16)
+    dy = cot + rms_pull(y_first, inv, datt_ref[...].astype(F32)).astype(BF16)
+    dy_ref[...] = tn(turn, dy).astype(BF16)
+
+
+def on_chip(kernel, operands, outs, scratch, flops, moved):
+    arrays, specs = [], []
+    for operand in operands:
+        array, shape, block = operand if isinstance(operand, tuple) else (operand, operand.shape, 0)
+        arrays.append(array)
+        specs.append(pl.BlockSpec(shape, lambda _, block=block: (0, block), pipeline_mode=pl.Buffered(1)))
+    return pl.pallas_call(
+        kernel,
+        grid=(1,),
+        in_specs=specs,
+        out_specs=tuple(pl.BlockSpec(shape, lambda _: (0, 0)) for shape in outs),
+        out_shape=tuple(jax.ShapeDtypeStruct(shape, BF16) for shape in outs),
+        scratch_shapes=[pltpu.VMEM(shape, BF16) for shape in scratch],
+        cost_estimate=pl.CostEstimate(flops=flops, bytes_accessed=moved, transcendentals=0),
+    )(*arrays)
+
+
+def gather_weights(shard):
+    return lax.all_gather(shard, "grid", axis=0, tiled=True)
+
+
+def exchange(rows, grid_size):
+    total, width = rows.shape
+    split = rows.reshape(grid_size, total // grid_size, width)
+    return lax.all_to_all(split, "grid", split_axis=0, concat_axis=0, tiled=True).reshape(
+        total, width
+    )
+
+
+def local_bands(tokens, cotangent, w_sqkv, w_so, w_gqkv, w_go, keep):
+    patches, groups, width = tokens.shape
+    grid_size = lax.axis_size("grid")
+    rows = patches * groups
+    head = width // H
+    position = lax.axis_index("grid")
+    weights = gather_weights(jnp.concatenate([w_sqkv, w_gqkv, w_so, w_go], axis=1))
+    full_sqkv = (weights, (width, 3 * width), 0)
+    full_gqkv = (weights, (width, 3 * width), 1)
+    full_so = (weights, (width, width), 6)
+    full_go = (weights, (width, width), 7)
+    keep_row = lax.dynamic_slice_in_dim(keep, position, 1, axis=0).astype(F32)
+    weight = width * width
+    product = 2 * rows * weight
+    wide, flat = (rows, 3 * width), (rows, width)
+
+    x = exchange(tokens.transpose(1, 0, 2).reshape(flat), grid_size)
+    qkv, y_first = on_chip(
+        partial(spatial_kernel, head),
+        (x, full_sqkv, full_so, keep_row),
+        (wide, flat),
+        (flat,),
+        5 * product,
+        8 * weight,
+    )
+    y_local = exchange(y_first, grid_size)
+    mixed, dy_local = on_chip(
+        partial(group_kernel, head, patches),
+        (y_local, cotangent.reshape(flat), full_gqkv, full_go),
+        (flat, flat),
+        (wide, flat, flat),
+        10 * product,
+        8 * weight,
+    )
+    dy = exchange(dy_local, grid_size)
+    (grad,) = on_chip(
+        partial(spatial_pull_kernel, head),
+        (dy, x, qkv, keep_row, full_so, full_sqkv),
+        (flat,),
+        (flat, wide),
+        6 * product,
+        8 * weight,
+    )
+    grad = exchange(grad, grid_size).reshape(groups, patches, width).transpose(1, 0, 2)
+    return mixed.reshape(patches, groups, width), grad
+
+
+def local(tokens, *rest):
+    if lax.axis_size("grid") == tokens.shape[1]:
+        return local_bands(tokens, *rest)
+    return local_any(tokens, *rest)
+
+
 def solution(mesh):
     placed = (
         P(("parts", "grid"), None, None),

time: 411 us -> 221 us (0.54)
  local copies, waits for them, and re-layouts: 178 us -> 8.09 us
  matrix products: 62.1 us -> 0 us
  Pallas kernels: 0 us -> 40 us
  blocking collectives: 12.8 us -> 38.8 us
  waiting for transfers between devices: 124 us -> 109 us
    unnamed x19 -> x2, local copies, waits for them, and re-layouts: 68.7 us -> 2.64 us
    dot_general x127 -> x0, matrix products: 62.1 us -> none  [the longest x48 19.4 us: pair_attention(): jnp.dot(probs, valued, preferred_element_type=jnp.float32)]
    all_to_all x4 -> x0, local copies, waits for them, and re-layouts: 43.8 us -> none  [the longest x1 42.5 us: local(): lax.all_to_all(stacked, 'grid', split_axis=2, concat_axis=1, tiled=True)]
    pallas_call x0 -> x3, Pallas kernels: none -> 40 us  [on_chip(): pl.pallas_call(kernel, grid=(1,), in_specs=specs, out_specs=tuple((pl.Blo...]
    all_to_all x3 -> x1, waiting for transfers between devices: 51 us -> 11.2 us  [exchange(): lax.all_to_all(split, 'grid', split_axis=0, concat_axis=0, tiled=True)]
    reshape x9 -> x6, local copies, waits for them, and re-layouts: 44.1 us -> 5.45 us  [the longest x3 3.16 us: exchange(): split = rows.reshape(grid_size, total // grid_size, width)]
    all_gather x4 -> x1, waiting for transfers between devices: 70.7 us -> 97.7 us  [gather_weights(): return lax.all_gather(shard, 'grid', axis=0, tiled=True)]
    all_to_all x1 -> x3, blocking collectives: 12.8 us -> 38.8 us  [exchange(): lax.all_to_all(split, 'grid', split_axis=0, concat_axis=0, tiled=True)]
  transfers between devices with their start and end apart: 7 -> 2, of which waited for: 4 -> 2; matrix products, arithmetic and copies ran while one was open for 45% -> 2% of each run, Pallas kernels for 0% -> 0%
where the time goes in v1:
time: 221 us; the launch traced here: 220 us
  waiting for transfers between devices  109 us (49%)
  Pallas kernels  40 us (18%)
  blocking collectives  38.8 us (18%)
  between operations  14.1 us (6%)
  local copies, waits for them, and re-layouts  8.09 us (4%)
  starting transfers between devices  7.36 us (3%)
  other arithmetic  3.1 us (1%)
    all_gather x1, waiting for transfers between devices, gather_weights(): return lax.all_gather(shard, 'grid', axis=0, tiled=True)  97.7 us
    pallas_call x3, Pallas kernels, on_chip(): pl.pallas_call(kernel, grid=(1,), in_specs=specs, out_specs=tuple((pl.Blo...  40 us
    all_to_all x3, blocking collectives, exchange(): lax.all_to_all(split, 'grid', split_axis=0, concat_axis=0, tiled=True)  38.8 us
    all_to_all x1, waiting for transfers between devices, exchange(): lax.all_to_all(split, 'grid', split_axis=0, concat_axis=0, tiled=True)  11.2 us
    all_to_all x1, starting transfers between devices, exchange(): lax.all_to_all(split, 'grid', split_axis=0, concat_axis=0, tiled=True)  7.33 us
  transfers between devices with their start and end apart: 2, of which 2 were waited for; matrix products, arithmetic and copies ran while one was open for 2% of the time, Pallas kernels for 0%

profile of v1, /device:TPU:0, one launch (start us, length us, event | category | flops | bytes accessed | tf_op | source)
XLA Modules:
  0.0 220.3 jit_solution(11074989634538980413)
XLA Ops:
  7.2 0.0 all-gather.2.cloned.1.call-start
  7.2 1.9 pad_maximum_fusion
  9.1 0.0 all-gather.2.cloned.1.call-update
  9.2 1.9 copy.14
  11.0 7.3 %all-to-all-start = ((bf16[32,4,1024]{2,1,0:T(4,128)(2,1)}), bf16[32,4,1024]{2,1,0:T(4,128)(2,1)S(1)}, u32[]{:S(2)}, u32[]{:S(2)}) async-start(bf16[32,4,1024]{2,1,0:T(4,128)(2,1)} %bitcast.5), calls=%async_computation | async-start | bytes 524288 | tf_op jit(solution)/shard_map/all_to_all | solution.py:289
  18.4 1.2 dynamic-slice_convert_fusion.keep_ref
  19.5 11.2 %all-to-all-done = bf16[32,4,1024]{2,1,0:T(4,128)(2,1)S(1)} async-done(((bf16[32,4,1024]{2,1,0:T(4,128)(2,1)}), bf16[32,4,1024]{2,1,0:T(4,128)(2,1)S(1)}, u32[]{:S(2)}, u32[]{:S(2)}) %all-to-all-start) | async-done | bytes 262176 | tf_op jit(solution)/shard_map/all_to_all | solution.py:289
  30.8 0.8 reshape.28.x_ref
  31.5 97.7 %all-gather.2.cloned.1.call-done.w_ref.w_so_ref.w_go_ref = bf16[1024,8192]{1,0:T(8,128)(2,1)} async-done(((bf16[32,8192]{1,0:T(8,128)(2,1)}), bf16[1024,8192]{1,0:T(8,128)(2,1)}) %all-gather.2.cloned.1.call-update) | async-done | bytes 16777232 | tf_op jit(solution)/shard_map/all_gather | solution.py:283
  129.2 9.3 %shard_map.86 = (bf16[128,3072]{1,0:T(8,128)(2,1)}, bf16[128,1024]{1,0:T(8,128)(2,1)}) custom-call(bf16[128,1024]{1,0:T(8,128)(2,1)} %reshape.28.x_ref, bf16[1024,8192]{1,0:T(8,128)(2,1)} %all-gather.2.cloned.1.call-done.w_ref.w_so_ref.w_go_ref, bf16[1024,8192]{1,0:T(8,128)(2,1)} %all-gather.2.cloned.1.call-done.w_ref.w_so_ref.w_go_ref, ...), custom_call_target="tpu_custom_call" | custom-call | flops 1342177280 | bytes 8388608 | tf_op jit(solution)/shard_map/pallas_call | solution.py:271
  138.5 1.1 reshape.29
  139.6 13.2 %all_to_all.20 = bf16[32,4,1024]{2,1,0:T(4,128)(2,1)S(1)} all-to-all(bf16[32,4,1024]{2,1,0:T(4,128)(2,1)S(1)} %reshape.29), channel_id=1, replica_groups=mesh['parts'=1,'grid'=32] {'grid'}, dimensions={0} | all-to-all | bytes 524288 | tf_op jit(solution)/shard_map/all_to_all | solution.py:289
  152.8 0.8 reshape.30.y_ref
  153.6 17.3 %shard_map.87 = (bf16[128,1024]{1,0:T(8,128)(2,1)}, bf16[128,1024]{1,0:T(8,128)(2,1)}) custom-call(bf16[128,1024]{1,0:T(8,128)(2,1)} %reshape.30.y_ref, bf16[128,1024]{1,0:T(8,128)(2,1)} %bitcast.7, bf16[1024,8192]{1,0:T(8,128)(2,1)} %all-gather.2.cloned.1.call-done.w_ref.w_so_ref.w_go_ref, ...), custom_call_target="tpu_custom_call" | custom-call | flops 2684354560 | bytes 8388608 | tf_op jit(solution)/shard_map/pallas_call | solution.py:271
  170.9 1.1 reshape.33
  171.9 12.8 %all_to_all.21 = bf16[32,4,1024]{2,1,0:T(4,128)(2,1)S(1)} all-to-all(bf16[32,4,1024]{2,1,0:T(4,128)(2,1)S(1)} %reshape.33), channel_id=1, replica_groups=mesh['parts'=1,'grid'=32] {'grid'}, dimensions={0} | all-to-all | bytes 524288 | tf_op jit(solution)/shard_map/all_to_all | solution.py:289
  184.7 0.8 reshape.34.dy_ref
  185.5 13.4 %shard_map.88 = bf16[128,1024]{1,0:T(8,128)(2,1)} custom-call(bf16[128,1024]{1,0:T(8,128)(2,1)} %reshape.34.dy_ref, bf16[128,1024]{1,0:T(8,128)(2,1)} %reshape.28.x_ref, bf16[128,3072]{1,0:T(8,128)(2,1)} %get-tuple-element.9.qkv_ref, f32[1,128]{1,0:T(1,128)} %dynamic-slice_convert_fusion.keep_ref, ...), custom_call_target="tpu_custom_call" | custom-call | flops 1610612736 | bytes 8388608 | tf_op jit(solution)/shard_map/pallas_call | solution.py:271
  198.9 1.1 reshape.35
  199.9 12.8 %all_to_all.22 = bf16[32,4,1024]{2,1,0:T(4,128)(2,1)S(1)} all-to-all(bf16[32,4,1024]{2,1,0:T(4,128)(2,1)S(1)} %reshape.35), channel_id=1, replica_groups=mesh['parts'=1,'grid'=32] {'grid'}, dimensions={0} | all-to-all | bytes 524288 | tf_op jit(solution)/shard_map/all_to_all | solution.py:289
  212.7 0.8 copy.12
Async XLA Ops:
  7.2 122.1 %all-gather.2.cloned.1.call-start = ((), (), s32[]{:S(2)}) async-start(), calls=%async_computation.4 | async-start | bytes 17301504 | tf_op jit(solution)/shard_map/all_gather | solution.py:283
  11.0 19.7 %all-to-all-start = ((bf16[32,4,1024]{2,1,0:T(4,128)(2,1)}), bf16[32,4,1024]{2,1,0:T(4,128)(2,1)S(1)}, u32[]{:S(2)}, u32[]{:S(2)}) async-start(bf16[32,4,1024]{2,1,0:T(4,128)(2,1)} %bitcast.5), calls=%async_computation | async-start | bytes 524288 | tf_op jit(solution)/shard_map/all_to_all | solution.py:289
Sparse Core Ops, SparseCore 0:
  10.8 118.3 all-gather.1

commit v2 on v1

--- a/solution.py
+++ b/solution.py
@@ -265,9 +265,9 @@
 def on_chip(kernel, operands, outs, scratch, flops, moved):
     arrays, specs = [], []
     for operand in operands:
-        array, shape, block = operand if isinstance(operand, tuple) else (operand, operand.shape, 0)
+        array, shape, block = operand if isinstance(operand, tuple) else (operand, operand.shape, (0,) * operand.ndim)
         arrays.append(array)
-        specs.append(pl.BlockSpec(shape, lambda _, block=block: (0, block), pipeline_mode=pl.Buffered(1)))
+        specs.append(pl.BlockSpec(shape, lambda _, block=block: block, pipeline_mode=pl.Buffered(1)))
     return pl.pallas_call(
         kernel,
         grid=(1,),
@@ -279,8 +279,146 @@
     )(*arrays)
 
 
+SPLIT = (2, 2, 2)
+
+
+def gather_kernel(shard_ref, full_ref, send_sem, recv_sem, own_sem):
+    count = lax.axis_size("grid")
+    ny, nx, nc = SPLIT
+    depth = count // (ny * nx * nc)
+    part = lax.axis_index("parts")
+    me = lax.axis_index("grid")
+    core, x, y, z = me % 2, (me // 2) % 2, (me // 4) % 2, me // 8
+    rows = shard_ref.shape[1]
+
+    def place(z, y, x, core):
+        return ((z * ny + y) * nx + x) * nc + core
+
+    def back(k):
+        return (z + depth - k) % depth
+
+    zs = [place((z + k) % depth, y, x, core) for k in range(depth)]
+    xp, yp, cp = place(z, y, 1 - x, core), place(z, 1 - y, x, core), place(z, y, x, 1 - core)
+    peers = zs[1:] + [xp, yp, cp]
+    barrier = pltpu.get_barrier_semaphore()
+    for peer in peers:
+        pl.semaphore_signal(
+            barrier, inc=1, device_id=(part, peer), device_id_type=pl.DeviceIdType.MESH
+        )
+    pl.semaphore_wait(barrier, len(peers))
+
+    slots, sent = {}, []
+
+    def slot(name):
+        return slots.setdefault(name, len(slots))
+
+    def region(half, owner):
+        return full_ref.at[half, pl.ds(pl.multiple_of(owner * rows, rows), rows), :]
+
+    def copy(name, half, owner, peer, source=None):
+        at = slot(name)
+        return pltpu.make_async_remote_copy(
+            src_ref=region(half, owner) if source is None else source,
+            dst_ref=region(half, owner),
+            send_sem=send_sem.at[at],
+            recv_sem=recv_sem.at[at],
+            device_id=(part, peer),
+            device_id_type=pl.DeviceIdType.MESH,
+        )
+
+    def send(name, half, owner, peer):
+        source = shard_ref.at[half] if name[1] == "own" else None
+        made = copy(name, half, owner, peer, source)
+        made.start()
+        sent.append(made)
+
+    def arrive(name, half, owner):
+        copy(name, half, owner, me).wait_recv()
+
+    keeps = []
+    for half in range(2):
+        for k in range(1, depth):
+            send(("z", "own", half, k), half, me, zs[k])
+    for half in range(2):
+        keep = pltpu.make_async_copy(shard_ref.at[half], region(half, me), own_sem.at[half])
+        keep.start()
+        keeps.append(keep)
+    order = ((("y", yp), ("x", xp)), (("x", xp), ("y", yp)))
+
+    def owner_of(half, k, first, second):
+        cross_y, cross_x = (first, second) if half == 0 else (second, first)
+        return place(back(k), 1 - y if cross_y else y, 1 - x if cross_x else x, core)
+
+    def spread_line(k):
+        tag = "own" if k == 0 else "line"
+        for half in range(2):
+            mine = owner_of(half, k, False, False)
+            send(("first", tag, half, k), half, mine, order[half][0][1])
+        for half in range(2):
+            mine = owner_of(half, k, False, False)
+            send(("second", tag, half, k, 0), half, mine, order[half][1][1])
+            send(("core", tag, half, k, 0, 0), half, mine, cp)
+
+    def spread_first(k):
+        tag = "own" if k == 0 else "line"
+        for half in range(2):
+            got = owner_of(half, k, True, False)
+            arrive(("first", tag, half, k), half, got)
+            send(("second", "far", half, k, 1), half, got, order[half][1][1])
+            send(("core", "far", half, k, 1, 0), half, got, cp)
+
+    def spread_second(k, first):
+        tag = "far" if first else ("own" if k == 0 else "line")
+        for half in range(2):
+            got = owner_of(half, k, bool(first), True)
+            arrive(("second", tag, half, k, first), half, got)
+            send(("core", "far", half, k, first, 1), half, got, cp)
+
+    spread_line(0)
+    for k in range(1, depth):
+        for half in range(2):
+            arrive(("z", "own", half, k), half, place(back(k), y, x, core))
+        spread_line(k)
+        spread_first(k - 1)
+        spread_second(k - 1, 0)
+    spread_first(depth - 1)
+    for k in range(depth - 1):
+        spread_second(k, 1)
+    spread_second(depth - 1, 0)
+    spread_second(depth - 1, 1)
+    for k in range(depth):
+        for first in range(2):
+            for second in range(2):
+                tag = "far" if first or second else ("own" if k == 0 else "line")
+                for half in range(2):
+                    cross_y, cross_x = (first, second) if half == 0 else (second, first)
+                    got = place(
+                        back(k), 1 - y if cross_y else y, 1 - x if cross_x else x, 1 - core
+                    )
+                    arrive(("core", tag, half, k, first, second), half, got)
+    for made in sent:
+        made.wait_send()
+    for keep in keeps:
+        keep.wait()
+
+
 def gather_weights(shard):
-    return lax.all_gather(shard, "grid", axis=0, tiled=True)
+    halves_, rows, columns = shard.shape
+    count = lax.axis_size("grid")
+    transfers = 2 * (count // 8 - 1) + 8 * (count // 8) + 4 * (count // 8)
+    transfers += 2 * (count // 8)
+    return pl.pallas_call(
+        gather_kernel,
+        in_specs=[pl.BlockSpec(memory_space=pltpu.VMEM)],
+        out_specs=pl.BlockSpec(memory_space=pl.ANY),
+        out_shape=jax.ShapeDtypeStruct((halves_, rows * count, columns), BF16),
+        scratch_shapes=[
+            pltpu.SemaphoreType.DMA((transfers,)),
+            pltpu.SemaphoreType.DMA((transfers,)),
+            pltpu.SemaphoreType.DMA((2,)),
+        ],
+        compiler_params=pltpu.CompilerParams(collective_id=0, has_side_effects=True),
+    )(shard)
 
 
 def exchange(rows, grid_size):
@@ -297,11 +435,12 @@
     rows = patches * groups
     head = width // H
     position = lax.axis_index("grid")
-    weights = gather_weights(jnp.concatenate([w_sqkv, w_gqkv, w_so, w_go], axis=1))
-    full_sqkv = (weights, (width, 3 * width), 0)
-    full_gqkv = (weights, (width, 3 * width), 1)
-    full_so = (weights, (width, width), 6)
-    full_go = (weights, (width, width), 7)
+    shards = [jnp.concatenate(pair, axis=1) for pair in ((w_sqkv, w_so), (w_gqkv, w_go))]
+    weights = gather_weights(jnp.stack(shards))
+    full_sqkv = (weights, (None, width, 3 * width), (0, 0, 0))
+    full_so = (weights, (None, width, width), (0, 0, 3))
+    full_gqkv = (weights, (None, width, 3 * width), (1, 0, 0))
+    full_go = (weights, (None, width, width), (1, 0, 3))
     keep_row = lax.dynamic_slice_in_dim(keep, position, 1, axis=0).astype(F32)
     weight = width * width
     product = 2 * rows * weight

time: 221 us -> 206 us (0.932)
  waiting for transfers between devices: 109 us -> 0.01 us
  Pallas kernels: 40 us -> 131 us
  blocking collectives: 38.8 us -> 54.9 us
  between operations: 14.1 us -> 0.67 us
    all_gather x1 -> x0, waiting for transfers between devices: 97.7 us -> none  [gather_weights(): return lax.all_gather(shard, 'grid', axis=0, tiled=True)]
    pallas_call x0 -> x1, Pallas kernels: none -> 91.4 us  [gather_weights(): pl.pallas_call(gather_kernel, in_specs=[pl.BlockSpec(memory_space=pltpu.V...]
    all_to_all x3, blocking collectives: 38.8 us -> 54.9 us  [exchange(): lax.all_to_all(split, 'grid', split_axis=0, concat_axis=0, tiled=True)]
    all_to_all x1, waiting for transfers between devices: 11.2 us -> 0.01 us  [exchange(): lax.all_to_all(split, 'grid', split_axis=0, concat_axis=0, tiled=True)]
  transfers between devices with their start and end apart: 2 -> 1, of which waited for: 2 -> 0; matrix products, arithmetic and copies ran while one was open for 2% -> 2% of each run, Pallas kernels for 0% -> 44%
where the time goes in v2:
time: 206 us
  Pallas kernels  131 us (64%)
  blocking collectives  54.9 us (27%)
  local copies, waits for them, and re-layouts  8.1 us (4%)
  starting transfers between devices  7.33 us (4%)
  other arithmetic  3.21 us (2%)
    pallas_call x1, Pallas kernels, gather_weights(): pl.pallas_call(gather_kernel, in_specs=[pl.BlockSpec(memory_space=pltpu.V...  91.4 us
    all_to_all x3, blocking collectives, exchange(): lax.all_to_all(split, 'grid', split_axis=0, concat_axis=0, tiled=True)  54.9 us
    pallas_call x3, Pallas kernels, on_chip(): pl.pallas_call(kernel, grid=(1,), in_specs=specs, out_specs=tuple((pl.Blo...  40 us
    all_to_all x1, starting transfers between devices, exchange(): lax.all_to_all(split, 'grid', split_axis=0, concat_axis=0, tiled=True)  7.33 us
  transfers between devices with their start and end apart: 1, of which 0 were waited for; matrix products, arithmetic and copies ran while one was open for 2% of the time, Pallas kernels for 44%

profile of v2, /device:TPU:0, one launch (start us, length us, event | category | flops | bytes accessed | tf_op | source)
XLA Modules:
  0.0 205.5 jit_solution(1470653560681512116)
XLA Ops:
  0.6 1.9 copy.14
  2.5 7.3 %all-to-all-start = ((bf16[32,4,1024]{2,1,0:T(4,128)(2,1)}), bf16[32,4,1024]{2,1,0:T(4,128)(2,1)S(1)}, u32[]{:S(2)}, u32[]{:S(2)}) async-start(bf16[32,4,1024]{2,1,0:T(4,128)(2,1)} %bitcast.9), calls=%async_computation | async-start | bytes 524288 | tf_op jit(solution)/shard_map/all_to_all | solution.py:427
  9.8 1.1 maximum_bitcast_fusion
  11.0 0.8 pad_maximum_fusion.shard_ref
  11.8 91.4 %shard_map.86.w_ref.w_so_ref.w_go_ref = bf16[2,1024,4096]{2,1,0:T(8,128)(2,1)} custom-call(bf16[2,32,4096]{2,1,0:T(8,128)(2,1)} %pad_maximum_fusion.shard_ref), custom_call_target="tpu_custom_call" | custom-call | tf_op jit(solution)/shard_map/pallas_call | solution.py:410
  103.2 1.2 dynamic-slice_convert_fusion.keep_ref
  104.4 0.0 all-to-all-done
  104.4 0.8 reshape.28.x_ref
  105.2 9.3 %shard_map.87 = (bf16[128,3072]{1,0:T(8,128)(2,1)}, bf16[128,1024]{1,0:T(8,128)(2,1)}) custom-call(bf16[128,1024]{1,0:T(8,128)(2,1)} %reshape.28.x_ref, bf16[2,1024,4096]{2,1,0:T(8,128)(2,1)} %shard_map.86.w_ref.w_so_ref.w_go_ref, bf16[2,1024,4096]{2,1,0:T(8,128)(2,1)} %shard_map.86.w_ref.w_so_ref.w_go_ref, f32[1,128]{1,0:T(1,128)} %dynamic-slice_convert_fusion.keep_ref), custom_call_target="tpu_custom_call" | custom-call | flops 1342177280 | bytes 8388608 | tf_op jit(solution)/shard_map/pallas_call | solution.py:271
  114.5 1.1 reshape.29
  115.5 29.3 %all_to_all.20 = bf16[32,4,1024]{2,1,0:T(4,128)(2,1)S(1)} all-to-all(bf16[32,4,1024]{2,1,0:T(4,128)(2,1)S(1)} %reshape.29), channel_id=1, replica_groups=mesh['parts'=1,'grid'=32] {'grid'}, dimensions={0} | all-to-all | bytes 524288 | tf_op jit(solution)/shard_map/all_to_all | solution.py:427
  144.8 0.8 reshape.30.y_ref
  145.6 17.3 %shard_map.88 = (bf16[128,1024]{1,0:T(8,128)(2,1)}, bf16[128,1024]{1,0:T(8,128)(2,1)}) custom-call(bf16[128,1024]{1,0:T(8,128)(2,1)} %reshape.30.y_ref, bf16[128,1024]{1,0:T(8,128)(2,1)} %bitcast.11, bf16[2,1024,4096]{2,1,0:T(8,128)(2,1)} %shard_map.86.w_ref.w_so_ref.w_go_ref, bf16[2,1024,4096]{2,1,0:T(8,128)(2,1)} %shard_map.86.w_ref.w_so_ref.w_go_ref), custom_call_target="tpu_custom_call" | custom-call | flops 2684354560 | bytes 8388608 | tf_op jit(solution)/shard_map/pallas_call | solution.py:271
  162.9 1.1 reshape.33
  164.0 12.8 %all_to_all.21 = bf16[32,4,1024]{2,1,0:T(4,128)(2,1)S(1)} all-to-all(bf16[32,4,1024]{2,1,0:T(4,128)(2,1)S(1)} %reshape.33), channel_id=1, replica_groups=mesh['parts'=1,'grid'=32] {'grid'}, dimensions={0} | all-to-all | bytes 524288 | tf_op jit(solution)/shard_map/all_to_all | solution.py:427
  176.7 0.8 reshape.34.dy_ref
  177.5 13.4 %shard_map.89 = bf16[128,1024]{1,0:T(8,128)(2,1)} custom-call(bf16[128,1024]{1,0:T(8,128)(2,1)} %reshape.34.dy_ref, bf16[128,1024]{1,0:T(8,128)(2,1)} %reshape.28.x_ref, bf16[128,3072]{1,0:T(8,128)(2,1)} %get-tuple-element.9.qkv_ref, f32[1,128]{1,0:T(1,128)} %dynamic-slice_convert_fusion.keep_ref, bf16[2,1024,4096]{2,1,0:T(8,128)(2,1)} %shard_map.86.w_ref.w_so_ref.w_go_ref, ...), custom_call_target="tpu_custom_call" | custom-call | flops 1610612736 | bytes 8388608 | tf_op jit(solution)/shard_map/pallas_call | solution.py:271
  190.9 1.1 reshape.35
  192.0 12.8 %all_to_all.22 = bf16[32,4,1024]{2,1,0:T(4,128)(2,1)S(1)} all-to-all(bf16[32,4,1024]{2,1,0:T(4,128)(2,1)S(1)} %reshape.35), channel_id=1, replica_groups=mesh['parts'=1,'grid'=32] {'grid'}, dimensions={0} | all-to-all | bytes 524288 | tf_op jit(solution)/shard_map/all_to_all | solution.py:427
  204.7 0.8 copy.12
Async XLA Ops:
  2.5 101.9 %all-to-all-start = ((bf16[32,4,1024]{2,1,0:T(4,128)(2,1)}), bf16[32,4,1024]{2,1,0:T(4,128)(2,1)S(1)}, u32[]{:S(2)}, u32[]{:S(2)}) async-start(bf16[32,4,1024]{2,1,0:T(4,128)(2,1)} %bitcast.9), calls=%async_computation | async-start | bytes 524288 | tf_op jit(solution)/shard_map/all_to_all | solution.py:427

commit v3 on v2

--- a/solution.py
+++ b/solution.py
@@ -289,7 +289,8 @@
     part = lax.axis_index("parts")
     me = lax.axis_index("grid")
     core, x, y, z = me % 2, (me // 2) % 2, (me // 4) % 2, me // 8
-    rows = shard_ref.shape[1]
+    rows, columns = shard_ref.shape
+    cuts = part_cuts(columns)
 
     def place(z, y, x, core):
         return ((z * ny + y) * nx + x) * nc + core
@@ -313,7 +314,12 @@
         return slots.setdefault(name, len(slots))
 
     def region(half, owner):
-        return full_ref.at[half, pl.ds(pl.multiple_of(owner * rows, rows), rows), :]
+        low, high = cuts[half]
+        return full_ref.at[pl.ds(pl.multiple_of(owner * rows, rows), rows), low:high]
+
+    def own(half):
+        low, high = cuts[half]
+        return shard_ref.at[:, low:high]
 
     def copy(name, half, owner, peer, source=None):
         at = slot(name)
@@ -327,7 +333,7 @@
         )
 
     def send(name, half, owner, peer):
-        source = shard_ref.at[half] if name[1] == "own" else None
+        source = own(half) if name[1] == "own" else None
         made = copy(name, half, owner, peer, source)
         made.start()
         sent.append(made)
@@ -335,14 +341,12 @@
     def arrive(name, half, owner):
         copy(name, half, owner, me).wait_recv()
 
-    keeps = []
-    for half in range(2):
-        for k in range(1, depth):
+    send(("cx", "own"), 2, me, xp)
+    for k in range(1, depth):
+        for half in range(2):
             send(("z", "own", half, k), half, me, zs[k])
-    for half in range(2):
-        keep = pltpu.make_async_copy(shard_ref.at[half], region(half, me), own_sem.at[half])
-        keep.start()
-        keeps.append(keep)
+    keep = pltpu.make_async_copy(shard_ref, full_ref.at[pl.ds(pl.multiple_of(me * rows, rows), rows), :], own_sem)
+    keep.start()
     order = ((("y", yp), ("x", xp)), (("x", xp), ("y", yp)))
 
     def owner_of(half, k, first, second):
@@ -374,17 +378,41 @@
             arrive(("second", tag, half, k, first), half, got)
             send(("core", "far", half, k, first, 1), half, got, cp)
 
+    across = place(z, y, 1 - x, core)
     spread_line(0)
+    send(("cy", "own", 0), 2, me, yp)
+    send(("ccore", "own", 0, 0, 0), 2, me, cp)
+    for k in range(1, depth):
+        send(("cz", "own", k, 0, 0), 2, me, zs[k])
+    arrive(("cx", "own"), 2, across)
+    send(("cy", "far", 1), 2, across, yp)
+    send(("ccore", "far", 0, 0, 1), 2, across, cp)
+    for k in range(1, depth):
+        send(("cz", "far", k, 0, 1), 2, across, zs[k])
+    spread_first(0)
+    for cross in range(2):
+        got = place(z, 1 - y, 1 - x if cross else x, core)
+        arrive(("cy", "far" if cross else "own", cross), 2, got)
+        send(("ccore", "far", 0, 1, cross), 2, got, cp)
+        for k in range(1, depth):
+            send(("cz", "far", k, 1, cross), 2, got, zs[k])
     for k in range(1, depth):
         for half in range(2):
             arrive(("z", "own", half, k), half, place(back(k), y, x, core))
         spread_line(k)
-        spread_first(k - 1)
         spread_second(k - 1, 0)
-    spread_first(depth - 1)
-    for k in range(depth - 1):
-        spread_second(k, 1)
+        if k > 1:
+            spread_second(k - 2, 1)
+        spread_first(k)
+    spread_second(depth - 2, 1)
     spread_second(depth - 1, 0)
+    for k in range(1, depth):
+        for cross_y in range(2):
+            for cross_x in range(2):
+                tag = "far" if cross_y or cross_x else "own"
+                got = place(back(k), 1 - y if cross_y else y, 1 - x if cross_x else x, core)
+                arrive(("cz", tag, k, cross_y, cross_x), 2, got)
+                send(("ccore", "far", k, cross_y, cross_x), 2, got, cp)
     spread_second(depth - 1, 1)
     for k in range(depth):
         for first in range(2):
@@ -396,26 +424,33 @@
                         back(k), 1 - y if cross_y else y, 1 - x if cross_x else x, 1 - core
                     )
                     arrive(("core", tag, half, k, first, second), half, got)
+                got = place(back(k), 1 - y if first else y, 1 - x if second else x, 1 - core)
+                tag = "far" if first or second or k else "own"
+                arrive(("ccore", tag, k, first, second), 2, got)
     for made in sent:
         made.wait_send()
-    for keep in keeps:
-        keep.wait()
+    keep.wait()
+
+
+def part_cuts(columns):
+    unit = columns // 32
+    return ((0, 13 * unit), (13 * unit, 26 * unit), (26 * unit, columns))
 
 
 def gather_weights(shard):
-    halves_, rows, columns = shard.shape
+    rows, columns = shard.shape
     count = lax.axis_size("grid")
-    transfers = 2 * (count // 8 - 1) + 8 * (count // 8) + 4 * (count // 8)
-    transfers += 2 * (count // 8)
+    depth = count // 8
+    transfers = (2 * (depth - 1) + 14 * depth) + (3 + 4 * (depth - 1) + 4 * depth)
     return pl.pallas_call(
         gather_kernel,
         in_specs=[pl.BlockSpec(memory_space=pltpu.VMEM)],
         out_specs=pl.BlockSpec(memory_space=pl.ANY),
-        out_shape=jax.ShapeDtypeStruct((halves_, rows * count, columns), BF16),
+        out_shape=jax.ShapeDtypeStruct((rows * count, columns), BF16),
         scratch_shapes=[
             pltpu.SemaphoreType.DMA((transfers,)),
             pltpu.SemaphoreType.DMA((transfers,)),
-            pltpu.SemaphoreType.DMA((2,)),
+            pltpu.SemaphoreType.DMA,
         ],
         compiler_params=pltpu.CompilerParams(collective_id=0, has_side_effects=True),
     )(shard)
@@ -435,12 +470,12 @@
     rows = patches * groups
     head = width // H
     position = lax.axis_index("grid")
-    shards = [jnp.concatenate(pair, axis=1) for pair in ((w_sqkv, w_so), (w_gqkv, w_go))]
-    weights = gather_weights(jnp.stack(shards))
-    full_sqkv = (weights, (None, width, 3 * width), (0, 0, 0))
-    full_so = (weights, (None, width, width), (0, 0, 3))
-    full_gqkv = (weights, (None, width, 3 * width), (1, 0, 0))
-    full_go = (weights, (None, width, width), (1, 0, 3))
+    second = lax.all_gather(jnp.concatenate([w_gqkv, w_go], axis=1), "grid", axis=0, tiled=True)
+    first = gather_weights(jnp.concatenate([w_sqkv, w_so], axis=1))
+    full_sqkv = (first, (width, 3 * width), (0, 0))
+    full_so = (first, (width, width), (0, 3))
+    full_gqkv = (second, (width, 3 * width), (0, 0))
+    full_go = (second, (width, width), (0, 3))
     keep_row = lax.dynamic_slice_in_dim(keep, position, 1, axis=0).astype(F32)
     weight = width * width
     product = 2 * rows * weight

time: 206 us -> 182 us (0.88)
  Pallas kernels: 131 us -> 103 us
  between operations: 0.67 us -> 14.1 us
  blocking collectives: 54.9 us -> 43.6 us
    pallas_call x1, Pallas kernels: 91.4 us -> 63.3 us  [gather_weights(): pl.pallas_call(gather_kernel, in_specs=[pl.BlockSpec(memory_space=pltpu.V...]
    all_to_all x3, blocking collectives: 54.9 us -> 43.6 us  [exchange(): lax.all_to_all(split, 'grid', split_axis=0, concat_axis=0, tiled=True)]
    concatenate x0 -> x2, other arithmetic: none -> 3.37 us  [the longest x1 1.69 us: local_bands(): first = gather_weights(jnp.concatenate([w_sqkv, w_so], axis=1))]
  transfers between devices with their start and end apart: 1 -> 2, of which waited for: 0 -> 0; matrix products, arithmetic and copies ran while one was open for 2% -> 4% of each run, Pallas kernels for 44% -> 40%
where the time goes in v3:
time: 182 us; the launch traced here: 181 us
  Pallas kernels  103 us (57%)
  blocking collectives  43.6 us (24%)
  between operations  14.1 us (8%)
  local copies, waits for them, and re-layouts  8.13 us (4%)
  starting transfers between devices  7.36 us (4%)
  other arithmetic  4.55 us (2%)
    pallas_call x1, Pallas kernels, gather_weights(): pl.pallas_call(gather_kernel, in_specs=[pl.BlockSpec(memory_space=pltpu.V...  63.3 us
    all_to_all x3, blocking collectives, exchange(): lax.all_to_all(split, 'grid', split_axis=0, concat_axis=0, tiled=True)  43.6 us
    pallas_call x3, Pallas kernels, on_chip(): pl.pallas_call(kernel, grid=(1,), in_specs=specs, out_specs=tuple((pl.Blo...  40.1 us
    all_to_all x1, starting transfers between devices, exchange(): lax.all_to_all(split, 'grid', split_axis=0, concat_axis=0, tiled=True)  7.33 us
  transfers between devices with their start and end apart: 2, of which 0 were waited for; matrix products, arithmetic and copies ran while one was open for 4% of the time, Pallas kernels for 40%

profile of v3, /device:TPU:0, one launch (start us, length us, event | category | flops | bytes accessed | tf_op | source)
XLA Modules:
  0.0 181.1 jit_solution(1565925064909255892)
XLA Ops:
  7.2 0.0 all-gather.2.cloned.1.call-start
  7.2 1.7 pad_maximum_fusion.1
  8.9 0.0 all-gather.2.cloned.1.call-update
  8.9 1.9 %copy.14 = bf16[4,32,1024]{2,0,1:T(4,128)(2,1)} copy(bf16[4,32,1024]{2,1,0:T(8,128)(2,1)} %param.7) | data formatting | bytes 524288 | tf_op args[0]
  10.8 7.3 %all-to-all-start = ((bf16[32,4,1024]{2,1,0:T(4,128)(2,1)}), bf16[32,4,1024]{2,1,0:T(4,128)(2,1)S(1)}, u32[]{:S(2)}, u32[]{:S(2)}) async-start(bf16[32,4,1024]{2,1,0:T(4,128)(2,1)} %bitcast.5), calls=%async_computation | async-start | bytes 524288 | tf_op jit(solution)/shard_map/all_to_all | solution.py:462
  18.1 1.7 pad_maximum_fusion.shard_ref
  19.8 63.3 %shard_map.86.w_ref.w_so_ref = bf16[1024,4096]{1,0:T(8,128)(2,1)} custom-call(bf16[32,4096]{1,0:T(8,128)(2,1)} %pad_maximum_fusion.shard_ref), custom_call_target="tpu_custom_call" | custom-call | tf_op jit(solution)/shard_map/pallas_call | solution.py:445
  83.1 1.2 dynamic-slice_convert_fusion.keep_ref
  84.3 0.0 all-to-all-done
  84.3 0.8 reshape.28.x_ref
  85.1 9.4 %shard_map.87 = (bf16[128,3072]{1,0:T(8,128)(2,1)}, bf16[128,1024]{1,0:T(8,128)(2,1)}) custom-call(bf16[128,1024]{1,0:T(8,128)(2,1)} %reshape.28.x_ref, bf16[1024,4096]{1,0:T(8,128)(2,1)} %shard_map.86.w_ref.w_so_ref, bf16[1024,4096]{1,0:T(8,128)(2,1)} %shard_map.86.w_ref.w_so_ref, f32[1,128]{1,0:T(1,128)} %dynamic-slice_convert_fusion.keep_ref), custom_call_target="tpu_custom_call" | custom-call | flops 1342177280 | bytes 8388608 | tf_op jit(solution)/shard_map/pallas_call | solution.py:271
  94.4 1.1 reshape.29
  95.5 17.2 %all_to_all.20 = bf16[32,4,1024]{2,1,0:T(4,128)(2,1)S(1)} all-to-all(bf16[32,4,1024]{2,1,0:T(4,128)(2,1)S(1)} %reshape.29), channel_id=1, replica_groups=mesh['parts'=1,'grid'=32] {'grid'}, dimensions={0} | all-to-all | bytes 524288 | tf_op jit(solution)/shard_map/all_to_all | solution.py:462
  112.7 0.8 reshape.30.y_ref
  113.5 0.0 all-gather.2.cloned.1.call-done.w_ref.w_go_ref
  113.5 17.3 %shard_map.88 = (bf16[128,1024]{1,0:T(8,128)(2,1)}, bf16[128,1024]{1,0:T(8,128)(2,1)}) custom-call(bf16[128,1024]{1,0:T(8,128)(2,1)} %reshape.30.y_ref, bf16[128,1024]{1,0:T(8,128)(2,1)} %bitcast.7, bf16[1024,4096]{1,0:T(8,128)(2,1)} %all-gather.2.cloned.1.call-done.w_ref.w_go_ref, bf16[1024,4096]{1,0:T(8,128)(2,1)} %all-gather.2.cloned.1.call-done.w_ref.w_go_ref), custom_call_target="tpu_custom_call" | custom-call | flops 2684354560 | bytes 8388608 | tf_op jit(solution)/shard_map/pallas_call | solution.py:271
  130.8 1.1 reshape.33
  131.9 13.6 %all_to_all.21 = bf16[32,4,1024]{2,1,0:T(4,128)(2,1)S(1)} all-to-all(bf16[32,4,1024]{2,1,0:T(4,128)(2,1)S(1)} %reshape.33), channel_id=1, replica_groups=mesh['parts'=1,'grid'=32] {'grid'}, dimensions={0} | all-to-all | bytes 524288 | tf_op jit(solution)/shard_map/all_to_all | solution.py:462
  145.5 0.8 reshape.34.dy_ref
  146.2 13.4 %shard_map.89 = bf16[128,1024]{1,0:T(8,128)(2,1)} custom-call(bf16[128,1024]{1,0:T(8,128)(2,1)} %reshape.34.dy_ref, bf16[128,1024]{1,0:T(8,128)(2,1)} %reshape.28.x_ref, bf16[128,3072]{1,0:T(8,128)(2,1)} %get-tuple-element.9.qkv_ref, f32[1,128]{1,0:T(1,128)} %dynamic-slice_convert_fusion.keep_ref, bf16[1024,4096]{1,0:T(8,128)(2,1)} %shard_map.86.w_ref.w_so_ref, ...), custom_call_target="tpu_custom_call" | custom-call | flops 1610612736 | bytes 8388608 | tf_op jit(solution)/shard_map/pallas_call | solution.py:271
  159.6 1.1 reshape.35
  160.7 12.8 %all_to_all.22 = bf16[32,4,1024]{2,1,0:T(4,128)(2,1)S(1)} all-to-all(bf16[32,4,1024]{2,1,0:T(4,128)(2,1)S(1)} %reshape.35), channel_id=1, replica_groups=mesh['parts'=1,'grid'=32] {'grid'}, dimensions={0} | all-to-all | bytes 524288 | tf_op jit(solution)/shard_map/all_to_all | solution.py:462
  173.5 0.8 copy.12
Async XLA Ops:
  7.2 106.3 %all-gather.2.cloned.1.call-start = ((), (), s32[]{:S(2)}) async-start(), calls=%async_computation.4 | async-start | bytes 8650752 | tf_op jit(solution)/shard_map/all_gather | solution.py:473
  10.8 73.5 %all-to-all-start = ((bf16[32,4,1024]{2,1,0:T(4,128)(2,1)}), bf16[32,4,1024]{2,1,0:T(4,128)(2,1)S(1)}, u32[]{:S(2)}, u32[]{:S(2)}) async-start(bf16[32,4,1024]{2,1,0:T(4,128)(2,1)} %bitcast.5), calls=%async_computation | async-start | bytes 524288 | tf_op jit(solution)/shard_map/all_to_all | solution.py:462
Sparse Core Ops, SparseCore 0:
  10.8 98.5 all-gather.1

commit v4 on v3

--- a/solution.py
+++ b/solution.py
@@ -161,12 +161,42 @@
     return tuple(qkv_ref[:, part * width + at : part * width + at + LANES] for part in range(3))
 
 
-def spatial_kernel(head, x_ref, w_ref, w_so_ref, keep_ref, qkv_ref, y_ref, att_ref):
+def fetch(full_ref, held_ref, sems, order):
+    width = held_ref.shape[2]
+    copies = []
+    for block in range(4):
+        columns = full_ref.at[:, block * width : (block + 1) * width]
+        copies.append(pltpu.make_async_copy(columns, held_ref.at[block], sems.at[block]))
+    for block in order:
+        copies[block].start()
+    return copies
+
+
+def project(normed, held_ref, copies, qkv_ref, tile):
+    width = held_ref.shape[2]
+    for part in range(3):
+        copies[part].wait()
+        for at in range(0, width, tile):
+            columns = slice(part * width + at, part * width + at + tile)
+            qkv_ref[:, columns] = nn(normed, held_ref[part, :, at : at + tile]).astype(BF16)
+
+
+def project_pull(dqkv_ref, held_ref, out_ref, tile):
+    width = held_ref.shape[2]
+    for at in range(0, width, tile):
+        total = nt(dqkv_ref[:, :width], held_ref[0, at : at + tile, :])
+        for part in range(1, 3):
+            columns = slice(part * width, (part + 1) * width)
+            total = total + nt(dqkv_ref[:, columns], held_ref[part, at : at + tile, :])
+        out_ref[:, at : at + tile] = total.astype(BF16)
+
+
+def spatial_kernel(head, x_ref, full_ref, keep_ref, qkv_ref, y_ref, att_ref, held_ref, sems):
+    copies = fetch(full_ref, held_ref, sems, (0, 1, 2, 3))
     width = x_ref.shape[1]
     _, normed = rms_parts(x_ref[...].astype(F32))
     tile = 512
-    for at in range(0, 3 * width, tile):
-        qkv_ref[:, at : at + tile] = nn(normed, w_ref[:, at : at + tile]).astype(BF16)
+    project(normed, held_ref, copies, qkv_ref, tile)
     rows = x_ref.shape[0]
     mask = jnp.broadcast_to(keep_ref[...], (rows, rows)) > 0.0
     selects = halves(head)
@@ -179,20 +209,23 @@
             parts.append(nn(probs.astype(BF16), valued))
         att_ref[:, block * LANES : (block + 1) * LANES] = merge(selects, parts)
     attended = att_ref[...]
+    copies[3].wait()
     for at in range(0, width, tile):
         y_ref[:, at : at + tile] = (
-            x_ref[:, at : at + tile].astype(F32) + nn(attended, w_so_ref[:, at : at + tile])
+            x_ref[:, at : at + tile].astype(F32) + nn(attended, held_ref[3, :, at : at + tile])
         ).astype(BF16)
 
 
 def spatial_pull_kernel(
-    head, dy_ref, x_ref, qkv_ref, keep_ref, w_so_ref, w_ref, out_ref, datt_ref, dqkv_ref
+    head, dy_ref, x_ref, qkv_ref, keep_ref, full_ref, out_ref, datt_ref, dqkv_ref, held_ref, sems
 ):
+    copies = fetch(full_ref, held_ref, sems, (3, 0, 1, 2))
     rows, width = x_ref.shape
     dy = dy_ref[...]
     tile = 512
+    copies[3].wait()
     for at in range(0, width, tile):
-        datt_ref[:, at : at + tile] = nt(dy, w_so_ref[at : at + tile, :]).astype(BF16)
+        datt_ref[:, at : at + tile] = nt(dy, held_ref[3, at : at + tile, :]).astype(BF16)
     mask = jnp.broadcast_to(keep_ref[...], (rows, rows)) > 0.0
     selects = halves(head)
     scale = head ** (-0.5)
@@ -210,16 +243,17 @@
             )
     wide = x_ref[...].astype(F32)
     inv, _ = rms_parts(wide)
-    dqkv = dqkv_ref[...]
-    for at in range(0, width, tile):
-        datt_ref[:, at : at + tile] = nt(dqkv, w_ref[at : at + tile, :]).astype(BF16)
+    for part in range(3):
+        copies[part].wait()
+    project_pull(dqkv_ref, held_ref, datt_ref, tile)
     first = rms_pull(wide, inv, datt_ref[...].astype(F32)).astype(BF16)
     out_ref[...] = dy + first
 
 
 def group_kernel(
-    head, patches, y_ref, c_ref, w_ref, w_go_ref, mixed_ref, dy_ref, qkv_ref, att_ref, datt_ref
+    head, patches, y_ref, c_ref, full_ref, mixed_ref, dy_ref, qkv_ref, att_ref, datt_ref, held_ref, sems
 ):
+    copies = fetch(full_ref, held_ref, sems, (0, 1, 2, 3))
     rows, width = y_ref.shape
     groups = rows // patches
     row = lax.broadcasted_iota(jnp.int32, (rows, rows), 0)
@@ -230,10 +264,10 @@
     inv, normed = rms_parts(y_first)
     cot = c_ref[...]
     tile = 512
-    for at in range(0, 3 * width, tile):
-        qkv_ref[:, at : at + tile] = nn(normed, w_ref[:, at : at + tile]).astype(BF16)
+    project(normed, held_ref, copies, qkv_ref, tile)
+    copies[3].wait()
     for at in range(0, width, tile):
-        datt_ref[:, at : at + tile] = nt(cot, w_go_ref[at : at + tile, :]).astype(BF16)
+        datt_ref[:, at : at + tile] = nt(cot, held_ref[3, at : at + tile, :]).astype(BF16)
     selects = halves(head)
     scale = head ** (-0.5)
     for block in range(width // LANES):
@@ -253,30 +287,31 @@
     attended = att_ref[...]
     for at in range(0, width, tile):
         mixed_ref[:, at : at + tile] = (
-            y_first[:, at : at + tile] + nn(attended, w_go_ref[:, at : at + tile])
+            y_first[:, at : at + tile] + nn(attended, held_ref[3, :, at : at + tile])
         ).astype(BF16)
-    dqkv = qkv_ref[...]
-    for at in range(0, width, tile):
-        datt_ref[:, at : at + tile] = nt(dqkv, w_ref[at : at + tile, :]).astype(BF16)
+    project_pull(qkv_ref, held_ref, datt_ref, tile)
     dy = cot + rms_pull(y_first, inv, datt_ref[...].astype(F32)).astype(BF16)
     dy_ref[...] = tn(turn, dy).astype(BF16)
 
 
-def on_chip(kernel, operands, outs, scratch, flops, moved):
-    arrays, specs = [], []
-    for operand in operands:
-        array, shape, block = operand if isinstance(operand, tuple) else (operand, operand.shape, (0,) * operand.ndim)
-        arrays.append(array)
-        specs.append(pl.BlockSpec(shape, lambda _, block=block: block, pipeline_mode=pl.Buffered(1)))
+def on_chip(kernel, weights, operands, outs, scratch, flops, moved):
+    specs = [
+        pl.BlockSpec(memory_space=pl.ANY)
+        if operand is weights
+        else pl.BlockSpec(operand.shape, lambda _: (0, 0), pipeline_mode=pl.Buffered(1))
+        for operand in operands
+    ]
+    width = weights.shape[0]
     return pl.pallas_call(
         kernel,
         grid=(1,),
         in_specs=specs,
         out_specs=tuple(pl.BlockSpec(shape, lambda _: (0, 0)) for shape in outs),
         out_shape=tuple(jax.ShapeDtypeStruct(shape, BF16) for shape in outs),
-        scratch_shapes=[pltpu.VMEM(shape, BF16) for shape in scratch],
+        scratch_shapes=[pltpu.VMEM(shape, BF16) for shape in scratch]
+        + [pltpu.VMEM((4, width, width), BF16), pltpu.SemaphoreType.DMA((4,))],
         cost_estimate=pl.CostEstimate(flops=flops, bytes_accessed=moved, transcendentals=0),
-    )(*arrays)
+    )(*operands)
 
 
 SPLIT = (2, 2, 2)
@@ -472,10 +507,6 @@
     position = lax.axis_index("grid")
     second = lax.all_gather(jnp.concatenate([w_gqkv, w_go], axis=1), "grid", axis=0, tiled=True)
     first = gather_weights(jnp.concatenate([w_sqkv, w_so], axis=1))
-    full_sqkv = (first, (width, 3 * width), (0, 0))
-    full_so = (first, (width, width), (0, 3))
-    full_gqkv = (second, (width, 3 * width), (0, 0))
-    full_go = (second, (width, width), (0, 3))
     keep_row = lax.dynamic_slice_in_dim(keep, position, 1, axis=0).astype(F32)
     weight = width * width
     product = 2 * rows * weight
@@ -484,7 +515,8 @@
     x = exchange(tokens.transpose(1, 0, 2).reshape(flat), grid_size)
     qkv, y_first = on_chip(
         partial(spatial_kernel, head),
-        (x, full_sqkv, full_so, keep_row),
+        first,
+        (x, first, keep_row),
         (wide, flat),
         (flat,),
         5 * product,
@@ -493,7 +525,8 @@
     y_local = exchange(y_first, grid_size)
     mixed, dy_local = on_chip(
         partial(group_kernel, head, patches),
-        (y_local, cotangent.reshape(flat), full_gqkv, full_go),
+        second,
+        (y_local, cotangent.reshape(flat), second),
         (flat, flat),
         (wide, flat, flat),
         10 * product,
@@ -502,7 +535,8 @@
     dy = exchange(dy_local, grid_size)
     (grad,) = on_chip(
         partial(spatial_pull_kernel, head),
-        (dy, x, qkv, keep_row, full_so, full_sqkv),
+        first,
+        (dy, x, qkv, keep_row, first),
         (flat,),
         (flat, wide),
         6 * product,

time: 182 us -> 181 us (level)
  no operation moved by 1% of the time
where the time goes in v4:
time: 181 us; the launch traced here: 180 us
  Pallas kernels  103 us (57%)
  blocking collectives  43.7 us (24%)
  between operations  14.1 us (8%)
  local copies, waits for them, and re-layouts  8.14 us (4%)
  starting transfers between devices  7.36 us (4%)
  other arithmetic  4.55 us (3%)
    pallas_call x1, Pallas kernels, gather_weights(): pl.pallas_call(gather_kernel, in_specs=[pl.BlockSpec(memory_space=pltpu.V...  63.3 us
    all_to_all x3, blocking collectives, exchange(): lax.all_to_all(split, 'grid', split_axis=0, concat_axis=0, tiled=True)  43.7 us
    pallas_call x3, Pallas kernels, on_chip(): pl.pallas_call(kernel, grid=(1,), in_specs=specs, out_specs=tuple((pl.Blo...  39.3 us
    all_to_all x1, starting transfers between devices, exchange(): lax.all_to_all(split, 'grid', split_axis=0, concat_axis=0, tiled=True)  7.33 us
  transfers between devices with their start and end apart: 2, of which 0 were waited for; matrix products, arithmetic and copies ran while one was open for 4% of the time, Pallas kernels for 40%

profile of v4, /device:TPU:0, one launch (start us, length us, event | category | flops | bytes accessed | tf_op | source)
XLA Modules:
  0.0 180.5 jit_solution(16665512414041548911)
XLA Ops:
  7.2 0.0 all-gather.2.cloned.1.call-start
  7.2 1.7 pad_maximum_fusion.1
  8.9 0.0 all-gather.2.cloned.1.call-update
  8.9 1.9 %copy.14 = bf16[4,32,1024]{2,0,1:T(4,128)(2,1)} copy(bf16[4,32,1024]{2,1,0:T(8,128)(2,1)} %param.7) | data formatting | bytes 524288 | tf_op args[0]
  10.8 7.3 %all-to-all-start = ((bf16[32,4,1024]{2,1,0:T(4,128)(2,1)}), bf16[32,4,1024]{2,1,0:T(4,128)(2,1)S(1)}, u32[]{:S(2)}, u32[]{:S(2)}) async-start(bf16[32,4,1024]{2,1,0:T(4,128)(2,1)} %bitcast.5), calls=%async_computation | async-start | bytes 524288 | tf_op jit(solution)/shard_map/all_to_all | solution.py:497
  18.1 1.7 pad_maximum_fusion.shard_ref
  19.8 63.3 %shard_map.86.full_ref = bf16[1024,4096]{1,0:T(8,128)(2,1)} custom-call(bf16[32,4096]{1,0:T(8,128)(2,1)} %pad_maximum_fusion.shard_ref), custom_call_target="tpu_custom_call" | custom-call | tf_op jit(solution)/shard_map/pallas_call | solution.py:480
  83.1 1.2 dynamic-slice_convert_fusion.keep_ref
  84.3 0.0 all-to-all-done
  84.3 0.8 reshape.28.x_ref
  85.1 9.2 %shard_map.87 = (bf16[128,3072]{1,0:T(8,128)(2,1)}, bf16[128,1024]{1,0:T(8,128)(2,1)}) custom-call(bf16[128,1024]{1,0:T(8,128)(2,1)} %reshape.28.x_ref, bf16[1024,4096]{1,0:T(8,128)(2,1)} %shard_map.86.full_ref, f32[1,128]{1,0:T(1,128)} %dynamic-slice_convert_fusion.keep_ref), custom_call_target="tpu_custom_call" | custom-call | flops 1342177280 | bytes 8388608 | tf_op jit(solution)/shard_map/pallas_call | solution.py:305
  94.3 1.1 reshape.29
  95.3 17.4 %all_to_all.20 = bf16[32,4,1024]{2,1,0:T(4,128)(2,1)S(1)} all-to-all(bf16[32,4,1024]{2,1,0:T(4,128)(2,1)S(1)} %reshape.29), channel_id=1, replica_groups=mesh['parts'=1,'grid'=32] {'grid'}, dimensions={0} | all-to-all | bytes 524288 | tf_op jit(solution)/shard_map/all_to_all | solution.py:497
  112.7 0.8 reshape.30.y_ref
  113.5 0.0 all-gather.2.cloned.1.call-done.full_ref
  113.5 17.1 %shard_map.88 = (bf16[128,1024]{1,0:T(8,128)(2,1)}, bf16[128,1024]{1,0:T(8,128)(2,1)}) custom-call(bf16[128,1024]{1,0:T(8,128)(2,1)} %reshape.30.y_ref, bf16[128,1024]{1,0:T(8,128)(2,1)} %bitcast.7, bf16[1024,4096]{1,0:T(8,128)(2,1)} %all-gather.2.cloned.1.call-done.full_ref), custom_call_target="tpu_custom_call" | custom-call | flops 2684354560 | bytes 8388608 | tf_op jit(solution)/shard_map/pallas_call | solution.py:305
  130.6 1.1 reshape.33
  131.6 13.6 %all_to_all.21 = bf16[32,4,1024]{2,1,0:T(4,128)(2,1)S(1)} all-to-all(bf16[32,4,1024]{2,1,0:T(4,128)(2,1)S(1)} %reshape.33), channel_id=1, replica_groups=mesh['parts'=1,'grid'=32] {'grid'}, dimensions={0} | all-to-all | bytes 524288 | tf_op jit(solution)/shard_map/all_to_all | solution.py:497
  145.2 0.8 reshape.34.dy_ref
  146.0 13.0 %shard_map.89 = bf16[128,1024]{1,0:T(8,128)(2,1)} custom-call(bf16[128,1024]{1,0:T(8,128)(2,1)} %reshape.34.dy_ref, bf16[128,1024]{1,0:T(8,128)(2,1)} %reshape.28.x_ref, bf16[128,3072]{1,0:T(8,128)(2,1)} %get-tuple-element.9.qkv_ref, f32[1,128]{1,0:T(1,128)} %dynamic-slice_convert_fusion.keep_ref, bf16[1024,4096]{1,0:T(8,128)(2,1)} %shard_map.86.full_ref), custom_call_target="tpu_custom_call" | custom-call | flops 1610612736 | bytes 8388608 | tf_op jit(solution)/shard_map/pallas_call | solution.py:305
  159.0 1.1 reshape.35
  160.1 12.8 %all_to_all.22 = bf16[32,4,1024]{2,1,0:T(4,128)(2,1)S(1)} all-to-all(bf16[32,4,1024]{2,1,0:T(4,128)(2,1)S(1)} %reshape.35), channel_id=1, replica_groups=mesh['parts'=1,'grid'=32] {'grid'}, dimensions={0} | all-to-all | bytes 524288 | tf_op jit(solution)/shard_map/all_to_all | solution.py:497
  172.9 0.8 copy.12
Async XLA Ops:
  7.2 106.3 %all-gather.2.cloned.1.call-start = ((), (), s32[]{:S(2)}) async-start(), calls=%async_computation.4 | async-start | bytes 8650752 | tf_op jit(solution)/shard_map/all_gather | solution.py:508
  10.8 73.5 %all-to-all-start = ((bf16[32,4,1024]{2,1,0:T(4,128)(2,1)}), bf16[32,4,1024]{2,1,0:T(4,128)(2,1)S(1)}, u32[]{:S(2)}, u32[]{:S(2)}) async-start(bf16[32,4,1024]{2,1,0:T(4,128)(2,1)} %bitcast.5), calls=%async_computation | async-start | bytes 524288 | tf_op jit(solution)/shard_map/all_to_all | solution.py:497
Sparse Core Ops, SparseCore 0:
  10.8 98.8 all-gather.1
